TPU v7x, 256 devices: a whole 4x4x8 slice. The times are simulated.
256 devices in a mesh: segment: 4 (over z_hi, core), dp: 16 (over z_lo, y), mp: 4 (over x).
Axes of the slice: x: 4, y: 4, z: 8 (z_hi: 2, z_lo: 4; z = z_hi * 4 + z_lo), core: 2. Of those that a mesh axis runs over, the one named last changes fastest.
Arguments:
- hidden: bfloat16 [384, 64, 4096], P(('segment', 'dp'))
- final_gain: bfloat16 [4096], replicated, may hold values from 0.099609375 to 1.8984375
- key_weight: bfloat16 [4096, 2048], P('dp', 'mp'), may hold values from -0.09375 to 0.09375
- value_weight: bfloat16 [4096, 2048], P('dp', 'mp'), may hold values from -0.09375 to 0.09375
- queries: bfloat16 [32, 128, 2048], P('dp', None, 'mp'), may hold values from -6 to 6
- context_grad: bfloat16 [32, 128, 2048], P('dp', None, 'mp'), may hold values from -384 to 384
- passage_count: int32 [32], replicated, may hold values from 4 to 16, as said below
- passage_slot: int32 [32, 16], replicated, may hold values from -1 to 287, as said below
- slot_question: int32 [32], replicated, may hold values from 0 to 31, as said below
Outputs:
- grad_hidden: bfloat16 [384, 64, 4096], P(('segment', 'dp'), 'mp')
Inputs may be any that keep to these rules, and one draw needn't show every extreme that they name: `passage_count`: the counts add up to 288, and some question has 16 passages. `passage_slot`: entry [q, j] is the slot holding passage j of question q for j below passage_count[q], and -1 beyond. Slots are numbered device by device in the order of the segment and dp indices, 6 to a device; only devices of the first three segment indices hold passages, each of their slots exactly one, and no slot is named twice. One device holds at most 1 passages of the questions served by the decoder rows of one dp index (rows 2 * c to 2 * c + 1 on dp index c), and one segment index at most 6 passages of one question; both bounds are reached. `slot_question`: A permutation.
All inputs are finite; a program needn't handle non-finite values.
Results may differ from a plain program's by a relative error of at most 0.015.
Values may be sent and summed in bfloat16 or wider, within the bound.
A program may use at most 128 MiB of HBM per device.

v0:
```python
import math

import jax
import jax.numpy as jnp
from jax import lax
from jax.sharding import PartitionSpec as P

HEAD_DIM = 64


EPSILON = 1e-06


def on_device(
    hidden,
    final_gain,
    key_weight,
    value_weight,
    queries,
    context_grad,
    passage_count,
    passage_slot,
    slot_question,
):
    segments = lax.axis_size("segment")
    columns = lax.axis_size("dp")
    tensor_ways = lax.axis_size("mp")
    segment_at = lax.axis_index("segment")
    column_at = lax.axis_index("dp")
    tensor_at = lax.axis_index("mp")
    slots_here = hidden.shape[0]
    seq_len = hidden.shape[1]
    model_width = hidden.shape[2]
    questions = passage_count.shape[0]
    most_passages = passage_slot.shape[1]
    q_here = queries.shape[0]
    target_len = queries.shape[1]
    encoders = (segments - 1) * columns
    per_device = (q_here * most_passages + encoders - 1) // encoders
    per_segment = (most_passages + segments - 2) // (segments - 1)
    inner_here = key_weight.shape[1]
    heads_here = inner_here // HEAD_DIM
    row_count = slots_here * seq_len
    scaling = 1.0 / math.sqrt(HEAD_DIM)
    key_full, value_full = (
        lax.all_gather(key_weight, "dp", axis=0, tiled=True),
        lax.all_gather(value_weight, "dp", axis=0, tiled=True),
    )

    def project(normed_rows, weight_full):
        return jnp.dot(normed_rows, weight_full, preferred_element_type=jnp.float32)

    def project_back(grad_rows, weight_full):
        return lax.dot_general(
            grad_rows, weight_full, (((1,), (1,)), ((), ())), preferred_element_type=jnp.float32
        )

    hidden_rows = hidden.reshape(row_count, model_width)
    gain_vec = final_gain.astype(jnp.float32)
    inv_rms = lax.rsqrt(
        jnp.mean(jnp.square(hidden_rows.astype(jnp.float32)), axis=-1, keepdims=True) + EPSILON
    )
    normed = (hidden_rows.astype(jnp.float32) * inv_rms * gain_vec).astype(jnp.bfloat16)
    key_rows = project(normed, key_full).astype(jnp.bfloat16)
    value_rows = project(normed, value_full).astype(jnp.bfloat16)
    packed = jnp.concatenate([key_rows, value_rows], axis=-1).reshape(
        slots_here, seq_len, 2 * inner_here
    )
    question_ids = jnp.arange(questions, dtype=jnp.int32)
    passage_ids = jnp.arange(most_passages, dtype=jnp.int32)
    home_row = jnp.sum(
        jnp.where(slot_question[None, :] == question_ids[:, None], question_ids[None, :], 0), axis=1
    )
    present = (passage_slot >= 0) & (passage_ids[None, :] < passage_count[:, None])
    local_ids = jnp.arange(slots_here, dtype=jnp.int32)
    my_slots = (segment_at * columns + column_at) * slots_here + local_ids
    matched = (passage_slot[None, :, :] == my_slots[:, None, None]) & present[None, :, :]
    holding = jnp.any(matched, axis=(1, 2))
    owner_question = jnp.sum(jnp.where(matched, question_ids[None, :, None], 0), axis=(1, 2))
    owner_row = jnp.sum(
        jnp.where(owner_question[:, None] == question_ids[None, :], home_row[None, :], 0), axis=1
    )
    target_column = owner_row // q_here
    earlier = (
        holding[None, :]
        & (target_column[None, :] == target_column[:, None])
        & (local_ids[None, :] < local_ids[:, None])
    )
    send_rank = jnp.sum(earlier.astype(jnp.int32), axis=1)
    send_pick = (
        holding[None, None, :]
        & (target_column[None, None, :] == jnp.arange(columns, dtype=jnp.int32)[:, None, None])
        & (send_rank[None, None, :] == jnp.arange(per_device, dtype=jnp.int32)[None, :, None])
    ).astype(jnp.bfloat16)
    outgoing = jnp.einsum(
        "gcl,lsx->gcsx", send_pick, packed, preferred_element_type=jnp.float32
    ).astype(jnp.bfloat16)
    incoming = lax.all_to_all(outgoing, "dp", split_axis=0, concat_axis=0, tiled=True)
    row_ids = column_at * q_here + jnp.arange(q_here, dtype=jnp.int32)
    my_questions = jnp.sum(
        jnp.where(row_ids[:, None] == question_ids[None, :], slot_question[None, :], 0), axis=1
    )
    is_mine = my_questions[:, None] == question_ids[None, :]
    row_slots = jnp.sum(
        jnp.where(is_mine[:, :, None], passage_slot[None, :, :], 0), axis=1
    ).reshape(-1)
    row_live = jnp.any(is_mine[:, :, None] & present[None, :, :], axis=1).reshape(-1)
    question_of = jnp.repeat(jnp.arange(q_here, dtype=jnp.int32), most_passages)
    segment_slots = columns * slots_here
    segment_of = row_slots // segment_slots
    column_key = row_slots % segment_slots
    source_of = column_key // slots_here
    on_segment = row_live & (segment_of == segment_at)
    ahead = on_segment[None, :] & (column_key[None, :] < column_key[:, None])
    segment_rank = jnp.sum(
        (ahead & (question_of[None, :] == question_of[:, None])).astype(jnp.int32), axis=1
    )
    device_rank = jnp.sum(
        (ahead & (source_of[None, :] == source_of[:, None])).astype(jnp.int32), axis=1
    )
    gather_pick = jnp.sum(
        (
            on_segment[:, None, None, None, None]
            & (
                question_of[:, None, None, None, None]
                == jnp.arange(q_here, dtype=jnp.int32)[None, :, None, None, None]
            )
            & (
                segment_rank[:, None, None, None, None]
                == jnp.arange(per_segment, dtype=jnp.int32)[None, None, :, None, None]
            )
            & (
                source_of[:, None, None, None, None]
                == jnp.arange(columns, dtype=jnp.int32)[None, None, None, :, None]
            )
            & (
                device_rank[:, None, None, None, None]
                == jnp.arange(per_device, dtype=jnp.int32)[None, None, None, None, :]
            )
        ).astype(jnp.int32),
        axis=0,
    ).astype(jnp.bfloat16)
    compact = jnp.einsum(
        "krgc,gcsx->krsx", gather_pick, incoming, preferred_element_type=jnp.float32
    ).astype(jnp.bfloat16)
    pooled = lax.all_gather(compact[None], "segment", axis=0, tiled=True)
    segment_counts = jnp.sum(
        (
            row_live[None, None, :]
            & (question_of[None, None, :] == jnp.arange(q_here, dtype=jnp.int32)[:, None, None])
            & (segment_of[None, None, :] == jnp.arange(segments, dtype=jnp.int32)[None, :, None])
        ).astype(jnp.int32),
        axis=2,
    )
    live_slots = (
        jnp.arange(per_segment, dtype=jnp.int32)[None, None, :] < segment_counts[:, :, None]
    )
    key_total = segments * per_segment * seq_len
    key_live = (
        jnp.broadcast_to(live_slots[:, :, :, None], (q_here, segments, per_segment, seq_len))
        .reshape(q_here, key_total)
        .astype(jnp.float32)
    )

    def head_pass(head_no):
        first_col = head_no * HEAD_DIM
        key_head = lax.dynamic_slice_in_dim(pooled, first_col, HEAD_DIM, 4)
        value_head = lax.dynamic_slice_in_dim(pooled, inner_here + first_col, HEAD_DIM, 4)
        query_head = lax.dynamic_slice_in_dim(queries, first_col, HEAD_DIM, 2)
        grad_head = lax.dynamic_slice_in_dim(context_grad, first_col, HEAD_DIM, 2)
        scores = jnp.einsum(
            "ktd,skrld->ktsrl", query_head, key_head, preferred_element_type=jnp.float32
        )
        scores = scores.reshape(q_here, target_len, key_total) * scaling
        weights = jnp.exp(scores) * key_live[:, None, :]
        attn_probs = weights / jnp.sum(weights, axis=-1, keepdims=True)
        probs_half = attn_probs.astype(jnp.bfloat16).reshape(
            q_here, target_len, segments, per_segment, seq_len
        )
        context = jnp.einsum(
            "ktsrl,skrld->ktd", probs_half, value_head, preferred_element_type=jnp.float32
        ).astype(jnp.bfloat16)
        row_delta = jnp.sum(
            grad_head.astype(jnp.float32) * context.astype(jnp.float32), axis=-1, keepdims=True
        )
        prob_grads = jnp.einsum(
            "ktd,skrld->ktsrl", grad_head, value_head, preferred_element_type=jnp.float32
        )
        prob_grads = prob_grads.reshape(q_here, target_len, key_total)
        score_grads = (attn_probs * (prob_grads - row_delta)).astype(jnp.bfloat16)
        score_grads = score_grads.reshape(q_here, target_len, segments, per_segment, seq_len)
        score_mine = lax.dynamic_index_in_dim(score_grads, segment_at, 2, keepdims=False)
        probs_mine = lax.dynamic_index_in_dim(probs_half, segment_at, 2, keepdims=False)
        key_grads = (
            jnp.einsum("ktrl,ktd->krld", score_mine, query_head, preferred_element_type=jnp.float32)
            * scaling
        ).astype(jnp.bfloat16)
        value_grads = jnp.einsum(
            "ktrl,ktd->krld", probs_mine, grad_head, preferred_element_type=jnp.float32
        ).astype(jnp.bfloat16)
        return (key_grads, value_grads)

    key_grads, value_grads = lax.map(head_pass, jnp.arange(heads_here, dtype=jnp.int32))
    grad_shape = (q_here, per_segment, seq_len, inner_here)
    key_grads = jnp.moveaxis(key_grads, 0, 3).reshape(grad_shape)
    value_grads = jnp.moveaxis(value_grads, 0, 3).reshape(grad_shape)
    my_share = jnp.concatenate([key_grads, value_grads], axis=-1)
    spread_back = jnp.einsum(
        "krgc,krsx->gcsx", gather_pick, my_share, preferred_element_type=jnp.float32
    ).astype(jnp.bfloat16)
    owner_back = lax.all_to_all(spread_back, "dp", split_axis=0, concat_axis=0, tiled=True)
    token_grads = jnp.einsum(
        "gcl,gcsx->slx", send_pick, owner_back, preferred_element_type=jnp.float32
    ).astype(jnp.bfloat16)
    grad_flat = token_grads.reshape(row_count, 2 * inner_here)
    my_rows = row_count // tensor_ways
    token_share = seq_len // tensor_ways
    normed_grad = lax.psum_scatter(
        (
            project_back(grad_flat[:, :inner_here], key_full)
            + project_back(grad_flat[:, inner_here:], value_full)
        ).astype(jnp.bfloat16),
        "mp",
        scatter_dimension=0,
        tiled=True,
    ).astype(jnp.float32)
    first_token = tensor_at * token_share
    states_mine = lax.dynamic_slice_in_dim(hidden, first_token, token_share, 1).astype(jnp.float32)
    states_mine = states_mine.transpose(1, 0, 2).reshape(my_rows, model_width)
    rms_mine = lax.dynamic_slice_in_dim(
        inv_rms.reshape(slots_here, seq_len, 1), first_token, token_share, 1
    )
    rms_mine = rms_mine.transpose(1, 0, 2).reshape(my_rows, 1)
    scaled = gain_vec * normed_grad
    hidden_grad = rms_mine * scaled - states_mine * rms_mine**3 * jnp.mean(
        states_mine * scaled, axis=-1, keepdims=True
    )
    hidden_grad = hidden_grad.reshape(token_share, slots_here, model_width).transpose(1, 0, 2)
    return hidden_grad.astype(jnp.bfloat16)


def solution(mesh):
    in_specs = (
        P(("segment", "dp"), None, None),
        P(),
        P("dp", "mp"),
        P("dp", "mp"),
        P("dp", None, "mp"),
        P("dp", None, "mp"),
        P(),
        P(),
        P(),
    )
    out_specs = P(("segment", "dp"), "mp", None)
    return jax.shard_map(
        on_device, mesh=mesh, in_specs=in_specs, out_specs=out_specs, check_vma=False
    )
```

profile of v0, /device:TPU:1, one launch (start us, length us, event | category | flops | bytes accessed | tf_op | source)
XLA Modules:
  0.0 518.2 jit_solution(18247863727032568012)
XLA Ops:
  8.7 2.6 multiply_reduce_fusion
  13.1 2.7 fusion.34
  15.8 75.3 %all-gather.7.cloned.1.call-done = bf16[4096,512]{1,0:T(8,128)(2,1)} async-done(((bf16[256,512]{1,0:T(8,128)(2,1)}), bf16[4096,512]{1,0:T(8,128)(2,1)}) %all-gather.7.cloned.1.call-update) | async-done | bytes 4194320 | tf_op jit(solution)/shard_map/all_gather | solution.py:47
  91.1 4.9 convolution_convert_fusion.1
  96.0 82.6 %all-gather.5.cloned.1.call-done = bf16[4096,512]{1,0:T(8,128)(2,1)} async-done(((bf16[256,512]{1,0:T(8,128)(2,1)}), bf16[4096,512]{1,0:T(8,128)(2,1)}) %all-gather.5.cloned.1.call-update) | async-done | bytes 4194320 | tf_op jit(solution)/shard_map/all_gather | solution.py:46
  178.6 4.0 convolution_convert_fusion.2
  183.7 2.5 copy.68
  186.2 5.6 %all-to-all-start = ((bf16[16,1,64,1024]{3,2,1,0:T(8,128)(2,1)}), bf16[16,1,64,1024]{3,2,1,0:T(8,128)(2,1)S(1)}, u32[]{:S(2)}, u32[]{:S(2)}) async-start(bf16[16,1,64,1024]{3,2,1,0:T(8,128)(2,1)} %copy.68), calls=%async_computation | async-start | bytes 4194304 | tf_op jit(solution)/shard_map/all_to_all | solution.py:98
  193.4 35.5 %all-to-all-done = bf16[16,1,64,1024]{3,2,1,0:T(8,128)(2,1)S(1)} async-done(((bf16[16,1,64,1024]{3,2,1,0:T(8,128)(2,1)}), bf16[16,1,64,1024]{3,2,1,0:T(8,128)(2,1)S(1)}, u32[]{:S(2)}, u32[]{:S(2)}) %all-to-all-start) | async-done | bytes 2097184 | tf_op jit(solution)/shard_map/all_to_all | solution.py:98
  228.9 1.5 fusion.44
  230.5 2.0 copy.70
  233.4 99.8 %all-gather.9.cloned.1.call-done = bf16[8,6,64,1024]{3,2,1,0:T(8,128)(2,1)} async-done(((bf16[2,6,64,1024]{3,2,1,0:T(8,128)(2,1)}), bf16[8,6,64,1024]{3,2,1,0:T(8,128)(2,1)}) %all-gather.9.cloned.1.call-update) | async-done | bytes 6291472 | tf_op jit(solution)/shard_map/all_gather | solution.py:146
  333.2 6.7 %copy.72 = bf16[4,2,6,64,1024]{4,3,2,0,1:T(8,128)(2,1)} copy(bf16[4,2,6,64,1024]{4,3,2,1,0:T(8,128)(2,1)} %bitcast.142) | data formatting | bytes 12582912
  339.9 57.2 %while.15 = (s32[]{:T(128)}, bf16[8,2,6,64,64]{4,3,2,1,0:T(8,128)(2,1)}, bf16[8,2,6,64,64]{4,3,2,1,0:T(8,128)(2,1)}, s32[8]{0:T(128)S(1)}, bf16[2,128,512]{1,2,0...) while((s32[]{:T(128)}, ...), condition=%wide.region_16.17_spmd.clone, body=%wide.region_13.16_spmd.clone.sunk | while | flops 178650624 | bytes 12167454 | solution.py:203
  341.1 1.6 fusion.113
  348.2 1.6 fusion.113
  355.4 1.6 fusion.113
  362.5 1.6 fusion.113
  369.7 1.6 fusion.113
  376.9 1.6 fusion.113
  384.0 1.6 fusion.113
  391.1 1.6 fusion.113
  397.1 2.4 copy.90
  400.6 2.4 copy.91
  403.0 1.8 reshape.671
  404.8 2.4 fusion.47
  408.4 51.3 %all_to_all.10 = bf16[16,1,64,1024]{3,2,1,0:T(8,128)(2,1)S(1)} all-to-all(bf16[16,1,64,1024]{3,2,1,0:T(8,128)(2,1)S(1)} %copy.78), channel_id=1, replica_groups=mesh['segment'=4,'dp'=16,'mp'=4] {'dp'}, dimensions={0} | all-to-all | bytes 4194304 | tf_op jit(solution)/shard_map/all_to_all | solution.py:211
  461.3 4.2 fusion.58
  465.5 3.5 add_convert_fusion
  470.3 2.3 copy.80
  472.6 1.7 reshape.658
  474.6 33.6 %reduce-scatter.2.cloned.1.call-done = bf16[96,4096]{1,0:T(8,128)(2,1)} async-done(((bf16[384,4096]{1,0:T(8,128)(2,1)}), bf16[96,4096]{1,0:T(8,128)(2,1)}) %reduce-scatter.2.cloned.1.call-update) | async-done | bytes 786448 | tf_op jit(solution)/shard_map/reduce_scatter | solution.py:218
  (169 shorter events, 55.1 us)
Async XLA Ops:
  6.5 6.6 %copy-start = (bf16[6,64,4096]{2,1,0:T(8,128)(2,1)S(1)}, bf16[6,64,4096]{2,1,0:T(8,128)(2,1)}, u32[]{:S(2)}) copy-start(bf16[6,64,4096]{2,1,0:T(8,128)(2,1)} %param.11) | copy-start | bytes 9437188
  6.5 4.9 copy-start.21
  6.5 5.0 copy-start.6
  6.5 5.0 copy-start.20
  6.5 84.5 %all-gather.7.cloned.1.call-start = ((), (), s32[]{:S(2)}) async-start(), calls=%async_computation.4 | async-start | bytes 4456448 | tf_op jit(solution)/shard_map/all_gather | solution.py:47
  7.3 171.3 %all-gather.5.cloned.1.call-start = ((), (), s32[]{:S(2)}) async-start(), calls=%async_computation.3 | async-start | bytes 4456448 | tf_op jit(solution)/shard_map/all_gather | solution.py:46
  11.3 4.5 copy-start.8
  11.6 4.2 copy-start.10
  11.8 4.0 copy-start.12
  12.3 3.5 copy-start.15
  15.8 162.8 %copy-start.2 = (bf16[384,4096]{1,0:T(8,128)(2,1)S(1)}, bf16[384,4096]{1,0:T(8,128)(2,1)}, u32[]{:S(2)}) copy-start(bf16[384,4096]{1,0:T(8,128)(2,1)} %fusion.34) | copy-start | bytes 9437188
  178.6 4.1 copy-start.13
  178.6 4.1 copy-start.16
  178.6 4.1 copy-start.18
  186.2 5.7 %copy-start.22 = (s32[32]{0:T(128)S(1)}, s32[32]{0:T(128)}, u32[]{:S(2)}) copy-start(s32[32]{0:T(128)} %param.19) | copy-start | bytes 388
  186.2 6.0 %copy-start.7 = (s32[32,16]{0,1:T(8,128)S(1)}, s32[32,16]{0,1:T(8,128)}, u32[]{:S(2)}) copy-start(s32[32,16]{0,1:T(8,128)} %param.18) | copy-start | bytes 6148
  186.2 6.2 %copy-start.11 = (pred[32,16]{0,1:T(8,128)(4,1)S(1)}, pred[32,16]{0,1:T(8,128)(4,1)}, u32[]{:S(2)}) copy-start(pred[32,16]{0,1:T(8,128)(4,1)} %copy-done.10) | copy-start | bytes 1540
  186.2 42.8 %all-to-all-start = ((bf16[16,1,64,1024]{3,2,1,0:T(8,128)(2,1)}), bf16[16,1,64,1024]{3,2,1,0:T(8,128)(2,1)S(1)}, u32[]{:S(2)}, u32[]{:S(2)}) async-start(bf16[16,1,64,1024]{3,2,1,0:T(8,128)(2,1)} %copy.68), calls=%async_computation | async-start | bytes 4194304 | tf_op jit(solution)/shard_map/all_to_all | solution.py:98
  191.8 141.4 %all-gather.9.cloned.1.call-start = ((), (), s32[]{:S(2)}) async-start(), calls=%async_computation.6 | async-start | bytes 7864320 | tf_op jit(solution)/shard_map/all_gather | solution.py:146
  230.5 2.3 copy-start.4
  230.5 2.5 copy-start.5
  232.5 275.6 %reduce-scatter.2.cloned.1.call-start = ((), (), s32[]{:S(2)}) async-start(), calls=%async_computation.5 | async-start | bytes 3932160 | tf_op jit(solution)/shard_map/reduce_scatter | solution.py:218
  408.4 51.3 %copy-start.14 = (pred[6]{0:T(512)(128)(4,1)S(1)}, pred[6]{0:T(512)(128)(4,1)}, u32[]{:S(2)}) copy-start(pred[6]{0:T(512)(128)(4,1)} %copy-done.12) | copy-start | bytes 22
  408.4 51.3 %copy-start.17 = (s32[6]{0:T(128)S(1)}, s32[6]{0:T(128)}, u32[]{:S(2)}) copy-start(s32[6]{0:T(128)} %copy-done.15) | copy-start | bytes 76
  408.4 51.3 %copy-start.19 = (pred[6]{0:T(512)(128)(4,1)S(1)}, pred[6]{0:T(512)(128)(4,1)}, u32[]{:S(2)}) copy-start(pred[6]{0:T(512)(128)(4,1)} %broadcast_compare_fusion) | copy-start | bytes 22
  461.3 4.2 copy-start.1
  472.6 1.7 copy-start.9
  508.1 1.5 copy-start.3
Sparse Core Ops, SparseCore 0:
  9.1 81.8 all-gather.6
  92.9 85.7 all-gather.4
  232.7 100.5 all-gather.8
  469.1 38.9 reduce-scatter.1
where the time goes:
time: 519 us; the launch traced here: 518 us
  waiting for transfers between devices  328 us (63%)
  matrix products  56.4 us (11%)
  blocking collectives  51.3 us (10%)
  local copies, waits for them, and re-layouts  43.2 us (8%)
  other arithmetic  14.6 us (3%)
  between operations  13.6 us (3%)
  starting transfers between devices  5.98 us (1%)
    all_gather x1, waiting for transfers between devices, on_device(): pooled = lax.all_gather(compact[None], 'segment', axis=0, tiled=True)  99.8 us
    all_gather x1, waiting for transfers between devices, on_device(): lax.all_gather(key_weight, 'dp', axis=0, tiled=True)  82.6 us
    all_gather x1, waiting for transfers between devices, on_device(): lax.all_gather(value_weight, 'dp', axis=0, tiled=True)  75.3 us
    all_to_all x1, blocking collectives, on_device(): lax.all_to_all(spread_back, 'dp', split_axis=0, concat_axis=0, tiled=True)  51.3 us
    all_to_all x1, waiting for transfers between devices, on_device(): lax.all_to_all(outgoing, 'dp', split_axis=0, concat_axis=0, tiled=True)  35.5 us
    reduce_scatter x1, waiting for transfers between devices, on_device(): lax.psum_scatter((project_back(grad_flat[:, :inner_here], key_full) + pro...  33.6 us
    dot_general x8, matrix products, head_pass(): jnp.einsum('ktd,skrld->ktsrl', query_head, key_head, preferred_element_ty...  13.2 us
    dynamic_slice x8, local copies, waits for them, and re-layouts, head_pass(): lax.dynamic_slice_in_dim(pooled, inner_here + first_col, HEAD_DIM, 4)  11.4 us
  transfers between devices with their start and end apart: 5, of which 5 were waited for; matrix products, arithmetic and copies ran while one was open for 4% of the time, Pallas kernels for 0%

commit v1 on v0

v1 whole, which is shorter than its diff:
```python
import functools
import math

import jax
import jax.numpy as jnp
from jax import lax
from jax.experimental import pallas as pl
from jax.experimental.pallas import tpu as pltpu
from jax.sharding import PartitionSpec as P

HEAD_DIM = 64
EPSILON = 1e-06
TINY = 1.2e-38
MESH = pl.DeviceIdType.MESH

ARRIVAL = (
    (3, 0), (1, 0), (0, 3), (0, 1), (2, 0), (3, 3), (3, 1), (1, 3), (1, 1), (0, 2), (2, 3), (2, 1), (3, 2), (1, 2), (2, 2),
)
FIRST_TABLE = sum(first * 4**k for k, (first, _) in enumerate(ARRIVAL))
SECOND_TABLE = sum(second * 4**k for k, (_, second) in enumerate(ARRIVAL))
OTHERS = len(ARRIVAL)
LAG = 2


def reader_kernel(
    owner, counts, slots, gain, hidden_hbm, key_shard, value_shard, query_shard, grad_shard,
    out,
    blocks, states, normed, total, kv_rows, score_buf, prob_grad_buf, stats, grad_rows, send_buf, recv_buf, sum_buf,
    local_sem, first_send, second_send, mate_send, block_recv, mate_recv,
    stat_send_y, stat_recv_y, stat_send_z, stat_recv_z, stat_send_mate, stat_recv_mate,
    ring_send, ring_recv,
):
    segment, column, x = lax.axis_index("segment"), lax.axis_index("dp"), lax.axis_index("mp")
    z_hi, core = lax.div(segment, 2), lax.rem(segment, 2)
    z_lo, y = lax.div(column, 4), lax.rem(column, 4)
    z_next, z_prev = lax.rem(z_lo + 1, 4), lax.rem(z_lo + 3, 4)
    flip_next, flip_prev = lax.div(z_lo + 1, 4), 1 - lax.div(z_lo + 3, 4)
    y_up = (segment, z_lo * 4 + lax.rem(y + 1, 4), x)
    y_down = (segment, z_lo * 4 + lax.rem(y + 3, 4), x)
    z_up = (lax.rem(z_hi + flip_next, 2) * 2 + core, z_next * 4 + y, x)
    z_down = (lax.rem(z_hi + flip_prev, 2) * 2 + core, z_prev * 4 + y, x)
    mate = (z_hi * 2 + 1 - core, column, x)
    x_up = (segment, column, lax.rem(x + 1, 4))
    x_down = (segment, column, lax.rem(x + 3, 4))

    def by_core(if_zero, if_one):
        return tuple(a * (1 - core) + b * core for a, b in zip(if_zero, if_one))

    first_up, first_down = by_core(y_up, z_up), by_core(y_down, z_down)
    second_up, second_down = by_core(z_up, y_up), by_core(z_down, y_down)
    first_at = y * (1 - core) + z_lo * core
    second_at = z_lo * (1 - core) + y * core
    first_stride, second_stride = 1 + 3 * core, 4 - 3 * core
    other = 1 - core

    def remote(src, dst, send, recv, device):
        return pltpu.make_async_remote_copy(
            src_ref=src, dst_ref=dst, send_sem=send, recv_sem=recv, device_id=device, device_id_type=MESH
        )

    mine = pl.ds(2 * column, 2)
    local_copies = [
        pltpu.make_async_copy(src, dst, local_sem.at[k])
        for k, (src, dst) in enumerate(
            (
                (key_shard, blocks.at[0, 0, mine]),
                (value_shard, blocks.at[0, 1, mine]),
                (query_shard, blocks.at[1, 0, mine]),
                (grad_shard, blocks.at[1, 1, mine]),
                (hidden_hbm, states),
            )
        )
    ]
    for copy in local_copies:
        copy.start()
    barrier = pltpu.get_barrier_semaphore()
    for device in (y_up, y_down, z_up, z_down, mate, x_up, x_down):
        pl.semaphore_signal(barrier, inc=1, device_id=device, device_id_type=MESH)
    pl.semaphore_wait(barrier, 7)
    for copy in local_copies[:4]:
        copy.wait()

    def block_copy(kind, index, send, recv, device):
        ref = blocks.at[kind, core, index]
        return remote(ref, ref, send, recv, device)

    def to_first(kind, way, which, index):
        return block_copy(
            kind, index, first_send.at[kind, way, which], block_recv.at[kind, index], (first_up, first_down)[way]
        )

    def to_second(kind, lane, way, which, index):
        return block_copy(
            kind, index, second_send.at[kind, lane, way, which], block_recv.at[kind, index],
            (second_up, second_down)[way],
        )

    def to_mate(kind, index):
        return block_copy(kind, index, mate_send.at[kind, index], mate_recv.at[kind, index], mate)

    def send_own(kind):
        for half in range(2):
            for way in range(2):
                to_first(kind, way, half, 2 * column + half).start()
        for half in range(2):
            for way in range(2):
                to_second(kind, 0, way, half, 2 * column + half).start()

    send_own(0)
    local_copies[4].wait()

    slots_here = states.shape[0]
    width = states.shape[-1]
    parts = states.shape[1]
    token_share = states.shape[2]

    def norm_rows(step, carry):
        slot, part = lax.div(step, parts), lax.rem(step, parts)
        rows = states[slot, part].astype(jnp.float32)
        inv = lax.rsqrt(jnp.mean(rows * rows, axis=-1, keepdims=True) + EPSILON)
        scaled = (rows * inv * gain[...]).astype(jnp.bfloat16)
        at = pl.ds(pl.multiple_of(step * token_share, token_share), token_share)
        for shard in range(16):
            normed[shard, at, :] = scaled[:, shard * 256 : shard * 256 + 256]
        return carry

    lax.fori_loop(0, slots_here * parts, norm_rows, 0)

    def project(which, shard, first):
        weight = blocks[0, which, pl.ds(2 * shard, 2)].reshape(256, blocks.shape[-1])
        product = jnp.dot(normed[shard], weight, preferred_element_type=jnp.float32)
        total[which] = product if first else total[which] + product

    project(0, column, True)
    project(1, column, True)

    def table(power, first_base, second_base, stride_first, stride_second):
        first, second = lax.rem(lax.div(FIRST_TABLE, power), 4), lax.rem(lax.div(SECOND_TABLE, power), 4)
        shard = lax.rem(first_base + first, 4) * stride_first + lax.rem(second_base + second, 4) * stride_second
        return first, second, shard

    def next_power(power, k):
        return jnp.where(k == OTHERS - 1, 1, power * 4)

    def gather_step(step, powers):
        power, mate_power = powers
        kind, k = lax.div(step, OTHERS), lax.rem(step, OTHERS)

        @pl.when(step < 2 * OTHERS)
        def _():
            first, second, shard = table(power, first_at, second_at, first_stride, second_stride)
            for half in range(2):
                index = 2 * shard + half
                to_first(kind, 0, 0, index).wait_recv()

                @pl.when(second == 0)
                def _():
                    to_second(kind, first, 0, half, index).start()
                    to_second(kind, first, 1, half, index).start()

                @pl.when((second == 0) & (first == (3 if half == 0 else 1)))
                def _():
                    to_first(kind, half, 2, index).start()

                @pl.when(second == (3 if half == 0 else 1))
                def _():
                    to_second(kind, first, half, 2, index).start()

                to_mate(kind, index).start()

            @pl.when(kind == 0)
            def _():
                project(core, shard, False)

        @pl.when(step == OTHERS - 6)
        def _():
            send_own(1)

        back = step - LAG

        @pl.when(back >= 0)
        def _():
            mate_kind = lax.div(back, OTHERS)
            _, _, shard = table(mate_power, second_at, first_at, second_stride, first_stride)
            for half in range(2):
                ref = blocks.at[mate_kind, other, 2 * shard + half]
                remote(
                    ref, ref, mate_send.at[mate_kind, 2 * shard + half], mate_recv.at[mate_kind, 2 * shard + half], mate
                ).wait_recv()

            @pl.when(mate_kind == 0)
            def _():
                project(other, shard, False)

        new_mate = jnp.where(back >= 0, next_power(mate_power, lax.rem(jnp.maximum(back, 0), OTHERS)), mate_power)
        return next_power(power, k), new_mate

    lax.fori_loop(0, 2 * OTHERS + LAG, gather_step, (jnp.int32(1), jnp.int32(1)))

    for which in range(2):
        for slot in range(slots_here):
            kv_rows[which, slot] = total[which, slot * 64 : slot * 64 + 64, :].astype(jnp.bfloat16)

    lane = lax.broadcasted_iota(jnp.int32, (64, 128), 1)
    left = lane < HEAD_DIM
    left_half = left.astype(jnp.float32).astype(jnp.bfloat16)
    right_half = (1.0 - left.astype(jnp.float32)).astype(jnp.bfloat16)
    pairs = kv_rows.shape[-1] // 128
    scaling = 1.0 / math.sqrt(HEAD_DIM)
    across = (((1,), (1,)), ((), ()))

    def both_heads(top, bottom):
        return jnp.concatenate([jnp.broadcast_to(top, (64, 128)), jnp.broadcast_to(bottom, (64, 128))], axis=0)

    me = segment * 16 + column

    def scores_of(slot, carry):
        row = owner[slots_here + slot]
        sums, deltas = [], []
        for pair in range(pairs):
            cols = slice(pair * 128, pair * 128 + 128)
            keys, values = kv_rows[0, slot, :, cols], kv_rows[1, slot, :, cols]
            key_pair = jnp.concatenate([keys * left_half, keys * right_half], axis=0)
            value_pair = jnp.concatenate([values * left_half, values * right_half], axis=0)
            queries = blocks[1, 0, row, :, cols]
            grads = blocks[1, 1, row, :, cols]
            scores = lax.dot_general(key_pair, queries, across, preferred_element_type=jnp.float32) * scaling
            prob_grads = lax.dot_general(value_pair, grads, across, preferred_element_type=jnp.float32)
            score_buf[slot, pair] = scores
            prob_grad_buf[slot, pair] = prob_grads
            weights = jnp.exp(scores)
            both = [jnp.sum(weights[k * 64 : k * 64 + 64], axis=0, keepdims=True) for k in range(2)]
            log_both = both_heads(*[jnp.log(jnp.maximum(b, TINY)) for b in both])
            moved = jnp.exp(scores - log_both) * prob_grads
            sums += both
            deltas += [jnp.sum(moved[k * 64 : k * 64 + 64], axis=0, keepdims=True) for k in range(2)]
        stats[me, slot] = jnp.concatenate(sums + deltas, axis=0).astype(jnp.bfloat16)
        return carry

    lax.fori_loop(0, slots_here, scores_of, 0)

    z = z_hi * 4 + z_lo
    half_slots = slots_here // 2
    halves = (pl.ds(0, half_slots), pl.ds(half_slots, half_slots))
    whole = pl.ds(0, slots_here)

    def piece(z_of, y_of, core_of):
        return (lax.div(z_of, 4) * 2 + core_of) * 16 + lax.rem(z_of, 4) * 4 + y_of

    def stat_copy(at, part, send, recv, device):
        ref = stats.at[at, part]
        return remote(ref, ref, send, recv, device)

    def y_piece(offset):
        return piece(z, lax.rem(y + offset, 4), core)

    def along_y(way, which, offset, part):
        return stat_copy(
            y_piece(offset), part, stat_send_y.at[way, which], stat_recv_y.at[way, which], (y_up, y_down)[way]
        )

    def share(z_of, y_of, part, which):
        at = piece(z_of, y_of, core)
        return stat_copy(
            at, part, stat_send_mate.at[z_of * 4 + y_of, which], stat_recv_mate.at[z_of * 4 + y_of, which], mate
        )

    def along_z(way, lane_y, distance, part):
        z_of = lax.rem(z + (8 - distance if way == 0 else distance), 8)
        at = piece(z_of, lax.rem(y + lane_y, 4), core)
        return stat_copy(
            at, part, stat_send_z.at[way, lane_y, distance], stat_recv_z.at[way, lane_y, distance],
            (z_up, z_down)[way],
        )

    along_y(0, 0, 0, whole).start()
    along_y(1, 0, 0, whole).start()
    along_z(0, 0, 0, whole).start()
    along_z(1, 0, 0, whole).start()
    share(z, y, whole, 0).start()
    for way, offset in ((0, 3), (1, 1)):
        along_y(way, 0, offset, whole).wait_recv()
        along_y(way, 1, offset, halves[way]).start()
        along_z(0, offset, 0, whole).start()
        along_z(1, offset, 0, whole).start()
        share(z, lax.rem(y + offset, 4), whole, 0).start()
    for way in range(2):
        along_y(way, 1, 2, halves[way]).wait_recv()
    along_z(0, 2, 0, whole).start()
    along_z(1, 2, 0, whole).start()
    share(z, lax.rem(y + 2, 4), whole, 0).start()
    for distance in (1, 2, 3, 4):
        for lane_y in (0, 3, 1, 2):
            y_of = lax.rem(y + lane_y, 4)
            for way in range(2):
                z_of = lax.rem(z + (8 - distance if way == 0 else distance), 8)
                along_z(way, lane_y, distance - 1, halves[way] if distance == 4 else whole).wait_recv()
                if distance < 4:
                    along_z(way, lane_y, distance, halves[way] if distance == 3 else whole).start()
                    share(z_of, y_of, whole, 0).start()
                else:
                    share(z_of, y_of, halves[way], way).start()

    def mate_stats(fn):
        def step(k, carry):
            z_of, y_of = lax.div(k, 4), lax.rem(k, 4)
            fn(z_of, y_of)
            return carry

        lax.fori_loop(0, 32, step, 0)

    def wait_mate(z_of, y_of, received):
        far = lax.rem(z_of - z + 8, 8) == 4

        def finish(copy):
            copy.wait_recv() if received else copy.wait_send()

        @pl.when(far)
        def _():
            for way in range(2):
                finish(share(z_of, y_of, halves[way], way))

        @pl.when(jnp.logical_not(far))
        def _():
            finish(share(z_of, y_of, whole, 0))

    mate_stats(functools.partial(wait_mate, received=True))

    def grads_of(slot, carry):
        question = owner[slot]
        row = owner[slots_here + slot]
        holds = question >= 0
        base = jnp.maximum(question, 0)
        count = counts[base]
        tiles = []
        for k in range(16):
            at = slots[base * 16 + k]
            tile = stats[lax.div(at, slots_here), lax.rem(at, slots_here)].astype(jnp.float32)
            tiles.append((tile[:8], tile[8:], k < count))
        zero = jnp.zeros((8, 128), jnp.float32)
        all_sum = zero
        for sums, _, live in tiles:
            all_sum = all_sum + jnp.where(live, sums, zero)
        log_sum = jnp.log(jnp.maximum(all_sum, TINY))
        delta = zero
        for sums, deltas, live in tiles:
            share_of = jnp.exp(jnp.log(jnp.maximum(sums, TINY)) - log_sum)
            delta = delta + jnp.where(live, share_of * deltas, zero)
        at = pl.ds(pl.multiple_of(slot * token_share, token_share), token_share)
        inner = kv_rows.shape[-1]
        for pair in range(pairs):
            cols = slice(pair * 128, pair * 128 + 128)
            heads = [2 * pair, 2 * pair + 1]
            log_both = both_heads(*[log_sum[h : h + 1] for h in heads])
            delta_both = both_heads(*[delta[h : h + 1] for h in heads])
            probs = jnp.exp(score_buf[slot, pair] - log_both)
            score_grads = (probs * (prob_grad_buf[slot, pair] - delta_both)).astype(jnp.bfloat16)
            queries = blocks[1, 0, row, :, cols]
            grads = blocks[1, 1, row, :, cols]
            key_grads = jnp.dot(score_grads, queries, preferred_element_type=jnp.float32) * scaling
            value_grads = jnp.dot(probs.astype(jnp.bfloat16), grads, preferred_element_type=jnp.float32)
            for offset, both in ((0, key_grads), (inner, value_grads)):
                merged = jnp.where(left, both[:64], both[64:])
                merged = jnp.where(holds, merged, jnp.zeros_like(merged)).astype(jnp.bfloat16)
                for part in range(parts):
                    grad_rows[part, at, offset + pair * 128 : offset + pair * 128 + 128] = merged[
                        part * token_share : part * token_share + token_share
                    ]
        return carry

    lax.fori_loop(0, slots_here, grads_of, 0)

    rows_half = slots_here * token_share // 2
    chunks = recv_buf.shape[2]
    chunk_width = recv_buf.shape[-1]
    tiles_here = chunk_width // 256

    def lhs(first, second):
        return jnp.concatenate([grad_rows[first], grad_rows[second]], axis=0)

    def back(rows, chunk, tile):
        index = pl.ds(2 * (chunk * tiles_here + tile), 2)
        inner = kv_rows.shape[-1]
        keys = blocks[0, 0, index].reshape(256, inner)
        values = blocks[0, 1, index].reshape(256, inner)
        return lax.dot_general(rows[:, :inner], keys, across, preferred_element_type=jnp.float32) + lax.dot_general(
            rows[:, inner:], values, across, preferred_element_type=jnp.float32
        )

    def ring(step, way, chunk):
        return remote(
            send_buf.at[step, way, chunk], recv_buf.at[step, way, chunk],
            ring_send.at[step, way, chunk], ring_recv.at[step, way, chunk], (x_up, x_down)[way],
        )

    def first_chunk(chunk, carry):
        rows = lhs(lax.rem(x + 3, 4), lax.rem(x + 1, 4))
        for tile in range(tiles_here):
            cols = slice(tile * 256, tile * 256 + 256)
            product = back(rows, chunk, tile).astype(jnp.bfloat16)
            send_buf[0, 0, chunk, :, cols] = product[:rows_half]
            send_buf[2, 1, chunk, :, cols] = product[rows_half : 2 * rows_half]
            send_buf[2, 0, chunk, :, cols] = product[2 * rows_half : 3 * rows_half]
            send_buf[0, 1, chunk, :, cols] = product[3 * rows_half :]
        ring(0, 0, chunk).start()
        ring(0, 1, chunk).start()
        return carry

    lax.fori_loop(0, chunks, first_chunk, 0)

    def pass_on(step, chunk):
        for way in range(2):
            ring(step - 1, way, chunk).wait_recv()
            send_buf[step, way, chunk] = (
                send_buf[step, way, chunk].astype(jnp.float32) + recv_buf[step - 1, way, chunk].astype(jnp.float32)
            ).astype(jnp.bfloat16)
            ring(step, way, chunk).start()

    def second_chunk(chunk, carry):
        rows = lhs(lax.rem(x + 2, 4), x)
        for tile in range(tiles_here):
            cols = slice(tile * 256, tile * 256 + 256)
            product = back(rows, chunk, tile).astype(jnp.bfloat16)
            send_buf[1, 0, chunk, :, cols] = product[:rows_half]
            send_buf[1, 1, chunk, :, cols] = product[rows_half : 2 * rows_half]
            sum_buf[chunk, :, cols] = product[2 * rows_half :].astype(jnp.float32)
        pass_on(1, chunk)
        return carry

    lax.fori_loop(0, chunks, second_chunk, 0)

    def third_chunk(chunk, carry):
        pass_on(2, chunk)
        return carry

    lax.fori_loop(0, chunks, third_chunk, 0)

    def last_chunk(chunk, carry):
        for way in range(2):
            ring(2, way, chunk).wait_recv()
            at = slice(way * rows_half, way * rows_half + rows_half)
            sum_buf[chunk, at] = sum_buf[chunk, at] + recv_buf[2, way, chunk].astype(jnp.float32)
        return carry

    lax.fori_loop(0, chunks, last_chunk, 0)

    def finish_slot(slot, carry):
        at = pl.ds(pl.multiple_of(slot * token_share, token_share), token_share)
        rows = states[slot, x].astype(jnp.float32)
        inv = lax.rsqrt(jnp.mean(rows * rows, axis=-1, keepdims=True) + EPSILON)
        scaled = gain[...] * jnp.concatenate([sum_buf[c, at, :] for c in range(chunks)], axis=-1)
        mean = jnp.mean(rows * scaled, axis=-1, keepdims=True)
        out[slot] = (inv * scaled - rows * (inv * inv * inv) * mean).astype(jnp.bfloat16)
        return carry

    lax.fori_loop(0, slots_here, finish_slot, 0)

    for kind in range(2):
        for way in range(2):
            for which in range(3):
                to_first(kind, way, which, 2 * column).wait_send()

    def drain_second(k, carry):
        for kind in range(2):
            for way in range(2):
                for which in range(3):
                    to_second(kind, k, way, which, 2 * column).wait_send()
        return carry

    lax.fori_loop(0, 4, drain_second, 0)

    def drain_mate(k, power):
        _, _, shard = table(power, first_at, second_at, first_stride, second_stride)
        for kind in range(2):
            for half in range(2):
                to_mate(kind, 2 * shard + half).wait_send()
        return power * 4

    lax.fori_loop(0, OTHERS, drain_mate, jnp.int32(1))
    for way in range(2):
        along_y(way, 0, 0, whole).wait_send()
        along_y(way, 1, 0, halves[way]).wait_send()
        for lane_y in range(4):
            for distance in range(4):
                along_z(way, lane_y, distance, halves[way] if distance == 3 else whole).wait_send()
    mate_stats(functools.partial(wait_mate, received=False))

    def drain_ring(chunk, carry):
        for step in range(3):
            for way in range(2):
                ring(step, way, chunk).wait_send()
        return carry

    lax.fori_loop(0, chunks, drain_ring, 0)


def on_device(
    hidden, final_gain, key_weight, value_weight, queries, context_grad, passage_count, passage_slot, slot_question
):
    slots_here, seq_len, width = hidden.shape
    questions, most = passage_slot.shape
    tensor_ways = lax.axis_size("mp")
    token_share = seq_len // tensor_ways
    inner = key_weight.shape[1]
    me = lax.axis_index("segment") * lax.axis_size("dp") + lax.axis_index("dp")
    my_slots = me * slots_here + jnp.arange(slots_here, dtype=jnp.int32)
    question_ids = jnp.arange(questions, dtype=jnp.int32)
    present = (passage_slot >= 0) & (jnp.arange(most, dtype=jnp.int32)[None, :] < passage_count[:, None])
    matched = (passage_slot[None] == my_slots[:, None, None]) & present[None]
    question = jnp.max(jnp.where(matched, question_ids[None, :, None], -1), axis=(1, 2))
    row = jnp.sum(jnp.where(slot_question[None, :] == question[:, None], question_ids[None, :], 0), axis=1)
    owner = jnp.concatenate([question, row])
    slots = jnp.where(present, passage_slot, passage_slot[:, :1]).reshape(-1)
    rows = slots_here * seq_len
    chunks = 4
    rows_half = slots_here * token_share // 2
    smem, anywhere, vmem = (
        pl.BlockSpec(memory_space=pltpu.SMEM),
        pl.BlockSpec(memory_space=pl.ANY),
        pl.BlockSpec(memory_space=pltpu.VMEM),
    )
    half, single, dma = jnp.bfloat16, jnp.float32, pltpu.SemaphoreType.DMA
    shape_of = (2, 128, inner)
    return pl.pallas_call(
        reader_kernel,
        out_shape=jax.ShapeDtypeStruct((slots_here, token_share, width), half),
        in_specs=[smem, smem, smem, vmem] + [anywhere] * 5,
        out_specs=vmem,
        scratch_shapes=[
            pltpu.VMEM((2, 2, 32, 128, inner), half),
            pltpu.VMEM((slots_here, tensor_ways, token_share, width), half),
            pltpu.VMEM((16, rows, 256), half),
            pltpu.VMEM((2, rows, inner), single),
            pltpu.VMEM((2, slots_here, seq_len, inner), half),
            pltpu.VMEM((slots_here, inner // 128, 128, 128), single),
            pltpu.VMEM((slots_here, inner // 128, 128, 128), single),
            pltpu.VMEM((64, slots_here, 16, 128), half),
            pltpu.VMEM((tensor_ways, slots_here * token_share, 2 * inner), half),
            pltpu.VMEM((3, 2, chunks, rows_half, width // chunks), half),
            pltpu.VMEM((3, 2, chunks, rows_half, width // chunks), half),
            pltpu.VMEM((chunks, 2 * rows_half, width // chunks), single),
            dma((5,)),
            dma((2, 2, 3)),
            dma((2, 4, 2, 3)),
            dma((2, 32)),
            dma((2, 32)),
            dma((2, 32)),
            dma((2, 2)),
            dma((2, 2)),
            dma((2, 4, 4)),
            dma((2, 4, 4)),
            dma((32, 2)),
            dma((32, 2)),
            dma((3, 2, chunks)),
            dma((3, 2, chunks)),
        ],
        compiler_params=pltpu.CompilerParams(collective_id=0, has_side_effects=True, vmem_limit_bytes=60 << 20),
    )(
        owner,
        passage_count,
        slots,
        final_gain.astype(single)[None],
        hidden.reshape(slots_here, tensor_ways, token_share, width),
        key_weight.reshape(shape_of),
        value_weight.reshape(shape_of),
        queries,
        context_grad,
    )


def solution(mesh):
    in_specs = (
        P(("segment", "dp"), None, None),
        P(),
        P("dp", "mp"),
        P("dp", "mp"),
        P("dp", None, "mp"),
        P("dp", None, "mp"),
        P(),
        P(),
        P(),
    )
    return jax.shard_map(
        on_device, mesh=mesh, in_specs=in_specs, out_specs=P(("segment", "dp"), "mp", None), check_vma=False
    )
```

time: 519 us -> 127 us (0.24)
  waiting for transfers between devices: 328 us -> 0 us
  Pallas kernels: 0 us -> 118 us
  matrix products: 56.4 us -> 0 us
  blocking collectives: 51.3 us -> 0 us
  local copies, waits for them, and re-layouts: 43.2 us -> 3.5 us
  between operations: 13.6 us -> 0.01 us
  other arithmetic: 14.6 us -> 5.09 us
  starting transfers between devices: 5.98 us -> 0 us
    all_gather x3 -> x0, waiting for transfers between devices: 258 us -> none  [the longest x1 99.8 us: on_device(): pooled = lax.all_gather(compact[None], 'segment', axis=0, tiled=True)]
    pallas_call x0 -> x1, Pallas kernels: none -> 118 us  [on_device(): pl.pallas_call(reader_kernel, out_shape=jax.ShapeDtypeStruct((slots_here,...]
    dot_general x48 -> x0, matrix products: 56.4 us -> none  [the longest x8 13.2 us: head_pass(): jnp.einsum('ktd,skrld->ktsrl', query_head, key_head, preferred_element_ty...]
    all_to_all x1 -> x0, blocking collectives: 51.3 us -> none  [on_device(): lax.all_to_all(spread_back, 'dp', split_axis=0, concat_axis=0, tiled=True)]
    all_to_all x1 -> x0, waiting for transfers between devices: 35.5 us -> none  [on_device(): lax.all_to_all(outgoing, 'dp', split_axis=0, concat_axis=0, tiled=True)]
    reduce_scatter x1 -> x0, waiting for transfers between devices: 33.6 us -> none  [on_device(): lax.psum_scatter((project_back(grad_flat[:, :inner_here], key_full) + pro...]
    dynamic_slice x16 -> x0, local copies, waits for them, and re-layouts: 16.1 us -> none  [the longest x8 11.4 us: head_pass(): lax.dynamic_slice_in_dim(pooled, inner_here + first_col, HEAD_DIM, 4)]
    reshape x8 -> x1, local copies, waits for them, and re-layouts: 12 us -> 0.67 us  [on_device(): slots = jnp.where(present, passage_slot, passage_slot[:, :1]).reshape(-1)]
  transfers between devices with their start and end apart: 5 -> 0, of which waited for: 5 -> 0; matrix products, arithmetic and copies ran while one was open for 4% -> 0% of each run, Pallas kernels for 0% -> 0%
where the time goes in v1:
time: 127 us; the launch traced here: 126 us
  Pallas kernels  118 us (93%)
  other arithmetic  5.09 us (4%)
  local copies, waits for them, and re-layouts  3.5 us (3%)
    pallas_call x1, Pallas kernels, on_device(): pl.pallas_call(reader_kernel, out_shape=jax.ShapeDtypeStruct((slots_here,...  118 us

profile of v1, /device:TPU:1, one launch (start us, length us, event | category | flops | bytes accessed | tf_op | source)
XLA Modules:
  0.0 126.4 jit_solution(854809244811092206)
XLA Ops:
  0.0 0.7 slice_bitcast_fusion
  0.7 0.7 fusion
  1.4 1.0 select_reduce_fusion
  2.4 0.8 select_reduce_fusion.1
  3.2 0.6 pad_add_fusion.owner
  3.8 0.7 broadcast_select_fusion
  4.5 0.1 copy.15
  4.6 0.7 reshape.21.slots
  5.2 1.3 %broadcast_in_dim.56 = f32[4096]{0:T(1024)} convert(bf16[4096]{0:T(1024)(128)(2,1)} %param.10) | non-fusion elementwise | flops 4096 | bytes 24576 | tf_op jit(solution)/shard_map/broadcast_in_dim | solution.py:562
  6.5 117.8 %shard_map.91 = bf16[6,16,4096]{2,1,0:T(8,128)(2,1)} custom-call(s32[12]{0:T(128)} %pad_add_fusion.owner, s32[32]{0:T(128)} %counts.1, s32[512]{0:T(512)} %reshape.21.slots, f32[1,4096]{1,0:T(1,128)} %bitcast.9, bf16[6,4,16,4096]{3,2,1,0:T(8,128)(2,1)} %bitcast.6, bf16[2,128,512]{2,1,0:T(8,128)(2,1)} %bitcast.7, bf16[2,128,512]{2,1,0:T(8,128)(2,1)} %bitcast.8, ...), custom_call_target="tpu_custom_call" | custom-call | tf_op jit(solution)/shard_map/pallas_call | solution.py:524
  124.4 2.1 %copy.17 = bf16[6,16,4096]{2,1,0:T(8,128)(2,1)} copy(bf16[6,16,4096]{2,1,0:T(8,128)(2,1)} %shard_map.91) | data formatting | bytes 1572864
  (1 shorter events, 0.0 us)

commit v2 on v1

--- a/solution.py
+++ b/solution.py
@@ -20,12 +20,13 @@
 SECOND_TABLE = sum(second * 4**k for k, (_, second) in enumerate(ARRIVAL))
 OTHERS = len(ARRIVAL)
 LAG = 2
+NORM_STEPS = 8
 
 
 def reader_kernel(
-    owner, counts, slots, gain, hidden_hbm, key_shard, value_shard, query_shard, grad_shard,
+    counts, slots, slot_table, count_table, row_table, gain_half, hidden_hbm, key_shard, value_shard, query_shard, grad_shard,
     out,
-    blocks, states, normed, total, kv_rows, score_buf, prob_grad_buf, stats, grad_rows, send_buf, recv_buf, sum_buf,
+    owner, gain, blocks, states, normed, total, kv_rows, score_buf, prob_grad_buf, stats, grad_rows, send_buf, recv_buf, sum_buf,
     local_sem, first_send, second_send, mate_send, block_recv, mate_recv,
     stat_send_y, stat_recv_y, stat_send_z, stat_recv_z, stat_send_mate, stat_recv_mate,
     ring_send, ring_recv,
@@ -114,7 +115,11 @@
     parts = states.shape[1]
     token_share = states.shape[2]
 
-    def norm_rows(step, carry):
+    gain_rows = gain_half[...].astype(jnp.float32)
+    for k in range(gain_rows.shape[0]):
+        gain[:, k * 128 : k * 128 + 128] = gain_rows[k : k + 1]
+
+    def norm_rows(step):
         slot, part = lax.div(step, parts), lax.rem(step, parts)
         rows = states[slot, part].astype(jnp.float32)
         inv = lax.rsqrt(jnp.mean(rows * rows, axis=-1, keepdims=True) + EPSILON)
@@ -122,18 +127,23 @@
         at = pl.ds(pl.multiple_of(step * token_share, token_share), token_share)
         for shard in range(16):
             normed[shard, at, :] = scaled[:, shard * 256 : shard * 256 + 256]
-        return carry
-
-    lax.fori_loop(0, slots_here * parts, norm_rows, 0)
+
+    me = segment * 16 + column
+    question_ids = lax.broadcasted_iota(jnp.int32, slot_table.shape, 1)
+    passage_ids = lax.broadcasted_iota(jnp.int32, slot_table.shape, 0)
+    row_ids = lax.broadcasted_iota(jnp.int32, row_table.shape, 1)
+
+    def find_owner(slot):
+        found = (slot_table[...] == me * slots_here + slot) & (passage_ids < count_table[...])
+        question = jnp.max(jnp.where(found, question_ids, -1))
+        owner[slot] = question
+        owner[slots_here + slot] = jnp.max(jnp.where(row_table[...] == question, row_ids, 0))
 
     def project(which, shard, first):
         weight = blocks[0, which, pl.ds(2 * shard, 2)].reshape(256, blocks.shape[-1])
         product = jnp.dot(normed[shard], weight, preferred_element_type=jnp.float32)
         total[which] = product if first else total[which] + product
 
-    project(0, column, True)
-    project(1, column, True)
-
     def table(power, first_base, second_base, stride_first, stride_second):
         first, second = lax.rem(lax.div(FIRST_TABLE, power), 4), lax.rem(lax.div(SECOND_TABLE, power), 4)
         shard = lax.rem(first_base + first, 4) * stride_first + lax.rem(second_base + second, 4) * stride_second
@@ -142,60 +152,81 @@
     def next_power(power, k):
         return jnp.where(k == OTHERS - 1, 1, power * 4)
 
+    def own_table(power):
+        return table(power, first_at, second_at, first_stride, second_stride)
+
+    def mate_table(power):
+        return table(power, second_at, first_at, second_stride, first_stride)
+
+    def advance(power, done):
+        return jnp.where(done >= 0, next_power(power, lax.rem(jnp.maximum(done, 0), OTHERS)), power)
+
     def gather_step(step, powers):
-        power, mate_power = powers
-        kind, k = lax.div(step, OTHERS), lax.rem(step, OTHERS)
+        kind = lax.div(step, OTHERS)
+        arrived, ready, mate_ready = step - LAG, step - NORM_STEPS, step - NORM_STEPS - LAG
 
         @pl.when(step < 2 * OTHERS)
         def _():
-            first, second, shard = table(power, first_at, second_at, first_stride, second_stride)
+            first, second, shard = own_table(powers[0])
             for half in range(2):
                 index = 2 * shard + half
                 to_first(kind, 0, 0, index).wait_recv()
+
+                @pl.when((second == 0) & (first == (3 if half == 0 else 1)))
+                def _():
+                    to_first(kind, half, 2, index).start()
 
                 @pl.when(second == 0)
                 def _():
                     to_second(kind, first, 0, half, index).start()
                     to_second(kind, first, 1, half, index).start()
 
-                @pl.when((second == 0) & (first == (3 if half == 0 else 1)))
-                def _():
-                    to_first(kind, half, 2, index).start()
-
                 @pl.when(second == (3 if half == 0 else 1))
                 def _():
                     to_second(kind, first, half, 2, index).start()
 
                 to_mate(kind, index).start()
 
-            @pl.when(kind == 0)
-            def _():
-                project(core, shard, False)
-
         @pl.when(step == OTHERS - 6)
         def _():
             send_own(1)
 
-        back = step - LAG
-
-        @pl.when(back >= 0)
-        def _():
-            mate_kind = lax.div(back, OTHERS)
-            _, _, shard = table(mate_power, second_at, first_at, second_stride, first_stride)
+        @pl.when(arrived >= 0)
+        def _():
+            mate_kind = lax.div(arrived, OTHERS)
+            _, _, shard = mate_table(powers[1])
             for half in range(2):
                 ref = blocks.at[mate_kind, other, 2 * shard + half]
                 remote(
                     ref, ref, mate_send.at[mate_kind, 2 * shard + half], mate_recv.at[mate_kind, 2 * shard + half], mate
                 ).wait_recv()
 
-            @pl.when(mate_kind == 0)
-            def _():
-                project(other, shard, False)
-
-        new_mate = jnp.where(back >= 0, next_power(mate_power, lax.rem(jnp.maximum(back, 0), OTHERS)), mate_power)
-        return next_power(power, k), new_mate
-
-    lax.fori_loop(0, 2 * OTHERS + LAG, gather_step, (jnp.int32(1), jnp.int32(1)))
+        @pl.when(step < NORM_STEPS)
+        def _():
+            each = slots_here * parts // NORM_STEPS
+            for k in range(each):
+                norm_rows(step * each + k)
+
+        @pl.when(step < slots_here)
+        def _():
+            find_owner(step)
+
+        @pl.when(ready == 0)
+        def _():
+            project(0, column, True)
+            project(1, column, True)
+
+        @pl.when((ready >= 0) & (ready < OTHERS))
+        def _():
+            project(core, own_table(powers[2])[2], False)
+
+        @pl.when((mate_ready >= 0) & (mate_ready < OTHERS))
+        def _():
+            project(other, mate_table(powers[3])[2], False)
+
+        return tuple(advance(power, done) for power, done in zip(powers, (step, arrived, ready, mate_ready)))
+
+    lax.fori_loop(0, 2 * OTHERS + LAG, gather_step, (jnp.int32(1),) * 4)
 
     for which in range(2):
         for slot in range(slots_here):
@@ -211,8 +242,6 @@
 
     def both_heads(top, bottom):
         return jnp.concatenate([jnp.broadcast_to(top, (64, 128)), jnp.broadcast_to(bottom, (64, 128))], axis=0)
-
-    me = segment * 16 + column
 
     def scores_of(slot, carry):
         row = owner[slots_here + slot]
@@ -334,7 +363,7 @@
         count = counts[base]
         tiles = []
         for k in range(16):
-            at = slots[base * 16 + k]
+            at = slots[jnp.where(k < count, k, 0), base]
             tile = stats[lax.div(at, slots_here), lax.rem(at, slots_here)].astype(jnp.float32)
             tiles.append((tile[:8], tile[8:], k < count))
         zero = jnp.zeros((8, 128), jnp.float32)
@@ -498,19 +527,10 @@
     hidden, final_gain, key_weight, value_weight, queries, context_grad, passage_count, passage_slot, slot_question
 ):
     slots_here, seq_len, width = hidden.shape
-    questions, most = passage_slot.shape
     tensor_ways = lax.axis_size("mp")
     token_share = seq_len // tensor_ways
     inner = key_weight.shape[1]
-    me = lax.axis_index("segment") * lax.axis_size("dp") + lax.axis_index("dp")
-    my_slots = me * slots_here + jnp.arange(slots_here, dtype=jnp.int32)
-    question_ids = jnp.arange(questions, dtype=jnp.int32)
-    present = (passage_slot >= 0) & (jnp.arange(most, dtype=jnp.int32)[None, :] < passage_count[:, None])
-    matched = (passage_slot[None] == my_slots[:, None, None]) & present[None]
-    question = jnp.max(jnp.where(matched, question_ids[None, :, None], -1), axis=(1, 2))
-    row = jnp.sum(jnp.where(slot_question[None, :] == question[:, None], question_ids[None, :], 0), axis=1)
-    owner = jnp.concatenate([question, row])
-    slots = jnp.where(present, passage_slot, passage_slot[:, :1]).reshape(-1)
+    slots = passage_slot.T
     rows = slots_here * seq_len
     chunks = 4
     rows_half = slots_here * token_share // 2
@@ -523,10 +543,12 @@
     shape_of = (2, 128, inner)
     return pl.pallas_call(
         reader_kernel,
-        out_shape=jax.ShapeDtypeStruct((slots_here, token_share, width), half),
-        in_specs=[smem, smem, smem, vmem] + [anywhere] * 5,
+        out_shape=pltpu.VMEM((slots_here, token_share, width), half),
+        in_specs=[smem, smem] + [vmem] * 4 + [anywhere] * 5,
         out_specs=vmem,
         scratch_shapes=[
+            pltpu.SMEM((2 * slots_here,), jnp.int32),
+            pltpu.VMEM((1, width), single),
             pltpu.VMEM((2, 2, 32, 128, inner), half),
             pltpu.VMEM((slots_here, tensor_ways, token_share, width), half),
             pltpu.VMEM((16, rows, 256), half),
@@ -556,10 +578,12 @@
         ],
         compiler_params=pltpu.CompilerParams(collective_id=0, has_side_effects=True, vmem_limit_bytes=60 << 20),
     )(
-        owner,
         passage_count,
         slots,
-        final_gain.astype(single)[None],
+        slots,
+        passage_count[None],
+        slot_question[None],
+        final_gain.reshape(-1, 128),
         hidden.reshape(slots_here, tensor_ways, token_share, width),
         key_weight.reshape(shape_of),
         value_weight.reshape(shape_of),

time: 127 us -> 118 us (0.929)
  other arithmetic: 5.09 us -> 0 us
  local copies, waits for them, and re-layouts: 3.5 us -> 0.88 us
    broadcast_in_dim x1 -> x0, other arithmetic: 1.3 us -> none  [on_device(): final_gain.astype(single)[None]]
where the time goes in v2:
time: 118 us
  Pallas kernels  117 us (99%)
    pallas_call x1, Pallas kernels, on_device(): pl.pallas_call(reader_kernel, out_shape=pltpu.VMEM((slots_here, token_sha...  117 us

profile of v2, /device:TPU:1, one launch (start us, length us, event | category | flops | bytes accessed | tf_op | source)
XLA Modules:
  0.0 118.2 jit_solution(2488558104334073074)
XLA Ops:
  0.0 117.3 %shard_map.91 = bf16[6,16,4096]{2,1,0:T(8,128)(2,1)S(1)} custom-call(s32[32]{0:T(128)} %counts.1, s32[16,32]{1,0:T(8,128)} %bitcast.10, s32[16,32]{1,0:T(8,128)} %bitcast.11, s32[1,32]{1,0:T(1,128)} %bitcast.13, s32[1,32]{1,0:T(1,128)} %bitcast.14, bf16[32,128]{1,0:T(8,128)(2,1)} %bitcast.12, bf16[6,4,16,4096]{3,2,1,0:T(8,128)(2,1)} %bitcast.7, ...), custom_call_target="tpu_custom_call" | custom-call | tf_op jit(solution)/shard_map/pallas_call | solution.py:544
  117.3 0.9 copy.11

commit v3 on v2

--- a/solution.py
+++ b/solution.py
@@ -1,4 +1,3 @@
-import functools
 import math
 
 import jax
@@ -27,8 +26,8 @@
     counts, slots, slot_table, count_table, row_table, gain_half, hidden_hbm, key_shard, value_shard, query_shard, grad_shard,
     out,
     owner, gain, blocks, states, normed, total, kv_rows, score_buf, prob_grad_buf, stats, grad_rows, send_buf, recv_buf, sum_buf,
-    local_sem, first_send, second_send, mate_send, block_recv, mate_recv,
-    stat_send_y, stat_recv_y, stat_send_z, stat_recv_z, stat_send_mate, stat_recv_mate,
+    local_sem, block_send, mate_send, block_recv, mate_recv,
+    stat_send, stat_recv_z, stat_recv_y, stat_recv_far, stat_recv_mate,
     ring_send, ring_recv,
 ):
     segment, column, x = lax.axis_index("segment"), lax.axis_index("dp"), lax.axis_index("mp")
@@ -43,6 +42,11 @@
     mate = (z_hi * 2 + 1 - core, column, x)
     x_up = (segment, column, lax.rem(x + 1, 4))
     x_down = (segment, column, lax.rem(x + 3, 4))
+
+    z = z_hi * 4 + z_lo
+
+    def z_peer(z_of):
+        return (lax.div(z_of, 4) * 2 + core, lax.rem(z_of, 4) * 4 + y, x)
 
     def by_core(if_zero, if_one):
         return tuple(a * (1 - core) + b * core for a, b in zip(if_zero, if_one))
@@ -75,9 +79,9 @@
     for copy in local_copies:
         copy.start()
     barrier = pltpu.get_barrier_semaphore()
-    for device in (y_up, y_down, z_up, z_down, mate, x_up, x_down):
+    for device in [y_up, y_down, mate, x_up, x_down] + [z_peer(lax.rem(z + d, 8)) for d in range(1, 8)]:
         pl.semaphore_signal(barrier, inc=1, device_id=device, device_id_type=MESH)
-    pl.semaphore_wait(barrier, 7)
+    pl.semaphore_wait(barrier, 12)
     for copy in local_copies[:4]:
         copy.wait()
 
@@ -85,27 +89,22 @@
         ref = blocks.at[kind, core, index]
         return remote(ref, ref, send, recv, device)
 
-    def to_first(kind, way, which, index):
-        return block_copy(
-            kind, index, first_send.at[kind, way, which], block_recv.at[kind, index], (first_up, first_down)[way]
-        )
-
-    def to_second(kind, lane, way, which, index):
-        return block_copy(
-            kind, index, second_send.at[kind, lane, way, which], block_recv.at[kind, index],
-            (second_up, second_down)[way],
-        )
+    def to_first(kind, way, index):
+        return block_copy(kind, index, block_send.at[kind], block_recv.at[kind, index], (first_up, first_down)[way])
+
+    def to_second(kind, way, index):
+        return block_copy(kind, index, block_send.at[kind], block_recv.at[kind, index], (second_up, second_down)[way])
 
     def to_mate(kind, index):
-        return block_copy(kind, index, mate_send.at[kind, index], mate_recv.at[kind, index], mate)
+        return block_copy(kind, index, mate_send.at[kind], mate_recv.at[kind, lax.div(index, 2)], mate)
 
     def send_own(kind):
         for half in range(2):
             for way in range(2):
-                to_first(kind, way, half, 2 * column + half).start()
+                to_first(kind, way, 2 * column + half).start()
         for half in range(2):
             for way in range(2):
-                to_second(kind, 0, way, half, 2 * column + half).start()
+                to_second(kind, way, 2 * column + half).start()
 
     send_own(0)
     local_copies[4].wait()
@@ -170,20 +169,20 @@
             first, second, shard = own_table(powers[0])
             for half in range(2):
                 index = 2 * shard + half
-                to_first(kind, 0, 0, index).wait_recv()
+                to_first(kind, 0, index).wait_recv()
 
                 @pl.when((second == 0) & (first == (3 if half == 0 else 1)))
                 def _():
-                    to_first(kind, half, 2, index).start()
+                    to_first(kind, half, index).start()
 
                 @pl.when(second == 0)
                 def _():
-                    to_second(kind, first, 0, half, index).start()
-                    to_second(kind, first, 1, half, index).start()
+                    to_second(kind, 0, index).start()
+                    to_second(kind, 1, index).start()
 
                 @pl.when(second == (3 if half == 0 else 1))
                 def _():
-                    to_second(kind, first, half, 2, index).start()
+                    to_second(kind, half, index).start()
 
                 to_mate(kind, index).start()
 
@@ -195,11 +194,8 @@
         def _():
             mate_kind = lax.div(arrived, OTHERS)
             _, _, shard = mate_table(powers[1])
-            for half in range(2):
-                ref = blocks.at[mate_kind, other, 2 * shard + half]
-                remote(
-                    ref, ref, mate_send.at[mate_kind, 2 * shard + half], mate_recv.at[mate_kind, 2 * shard + half], mate
-                ).wait_recv()
+            ref = blocks.at[mate_kind, other, pl.ds(2 * shard, 2)]
+            remote(ref, ref, mate_send.at[mate_kind], mate_recv.at[mate_kind, shard], mate).wait_recv()
 
         @pl.when(step < NORM_STEPS)
         def _():
@@ -268,92 +264,79 @@
 
     lax.fori_loop(0, slots_here, scores_of, 0)
 
-    z = z_hi * 4 + z_lo
     half_slots = slots_here // 2
     halves = (pl.ds(0, half_slots), pl.ds(half_slots, half_slots))
     whole = pl.ds(0, slots_here)
 
-    def piece(z_of, y_of, core_of):
-        return (lax.div(z_of, 4) * 2 + core_of) * 16 + lax.rem(z_of, 4) * 4 + y_of
-
-    def stat_copy(at, part, send, recv, device):
+    def has_passages(z_of):
+        return (core == 0) | (z_of < 4)
+
+    def stat_copy(z_of, offset, part, recv, device):
+        at = (lax.div(z_of, 4) * 2 + core) * 16 + lax.rem(z_of, 4) * 4 + lax.rem(y + offset, 4)
         ref = stats.at[at, part]
-        return remote(ref, ref, send, recv, device)
-
-    def y_piece(offset):
-        return piece(z, lax.rem(y + offset, 4), core)
-
-    def along_y(way, which, offset, part):
-        return stat_copy(
-            y_piece(offset), part, stat_send_y.at[way, which], stat_recv_y.at[way, which], (y_up, y_down)[way]
-        )
-
-    def share(z_of, y_of, part, which):
-        at = piece(z_of, y_of, core)
-        return stat_copy(
-            at, part, stat_send_mate.at[z_of * 4 + y_of, which], stat_recv_mate.at[z_of * 4 + y_of, which], mate
-        )
-
-    def along_z(way, lane_y, distance, part):
-        z_of = lax.rem(z + (8 - distance if way == 0 else distance), 8)
-        at = piece(z_of, lax.rem(y + lane_y, 4), core)
-        return stat_copy(
-            at, part, stat_send_z.at[way, lane_y, distance], stat_recv_z.at[way, lane_y, distance],
-            (z_up, z_down)[way],
-        )
-
-    along_y(0, 0, 0, whole).start()
-    along_y(1, 0, 0, whole).start()
-    along_z(0, 0, 0, whole).start()
-    along_z(1, 0, 0, whole).start()
-    share(z, y, whole, 0).start()
-    for way, offset in ((0, 3), (1, 1)):
-        along_y(way, 0, offset, whole).wait_recv()
-        along_y(way, 1, offset, halves[way]).start()
-        along_z(0, offset, 0, whole).start()
-        along_z(1, offset, 0, whole).start()
-        share(z, lax.rem(y + offset, 4), whole, 0).start()
-    for way in range(2):
-        along_y(way, 1, 2, halves[way]).wait_recv()
-    along_z(0, 2, 0, whole).start()
-    along_z(1, 2, 0, whole).start()
-    share(z, lax.rem(y + 2, 4), whole, 0).start()
-    for distance in (1, 2, 3, 4):
-        for lane_y in (0, 3, 1, 2):
-            y_of = lax.rem(y + lane_y, 4)
-            for way in range(2):
-                z_of = lax.rem(z + (8 - distance if way == 0 else distance), 8)
-                along_z(way, lane_y, distance - 1, halves[way] if distance == 4 else whole).wait_recv()
-                if distance < 4:
-                    along_z(way, lane_y, distance, halves[way] if distance == 3 else whole).start()
-                    share(z_of, y_of, whole, 0).start()
-                else:
-                    share(z_of, y_of, halves[way], way).start()
-
-    def mate_stats(fn):
-        def step(k, carry):
-            z_of, y_of = lax.div(k, 4), lax.rem(k, 4)
-            fn(z_of, y_of)
-            return carry
-
-        lax.fori_loop(0, 32, step, 0)
-
-    def wait_mate(z_of, y_of, received):
-        far = lax.rem(z_of - z + 8, 8) == 4
-
-        def finish(copy):
-            copy.wait_recv() if received else copy.wait_send()
-
-        @pl.when(far)
-        def _():
-            for way in range(2):
-                finish(share(z_of, y_of, halves[way], way))
-
-        @pl.when(jnp.logical_not(far))
-        def _():
-            finish(share(z_of, y_of, whole, 0))
-
-    mate_stats(functools.partial(wait_mate, received=True))
+        return remote(ref, ref, stat_send, recv, device)
+
+    def along_z(z_of, device):
+        return stat_copy(z_of, 0, whole, stat_recv_z.at[z_of], device)
+
+    def along_y(way, z_of):
+        return stat_copy(z_of, 0, whole, stat_recv_y.at[way, z_of], (y_up, y_down)[way])
+
+    def to_far(way, z_of):
+        return stat_copy(z_of, (3, 1)[way], halves[way], stat_recv_far.at[z_of], (y_up, y_down)[way])
+
+    def share(z_of, offset):
+        return stat_copy(z_of, offset, whole, stat_recv_mate, mate)
+
+    @pl.when(has_passages(z))
+    def _():
+        for distance in (4, 3, 5, 2, 6, 1, 7):
+            along_z(z, z_peer(lax.rem(z + distance, 8))).start()
+
+    order = (0, 7, 1, 6, 2, 5, 3, 4)
+
+    def z_of_turn(turn):
+        return lax.rem(z + order[turn], 8)
+
+    for turn in range(len(order) + 2):
+        if turn < len(order):
+            z_new = z_of_turn(turn)
+
+            @pl.when(has_passages(z_new))
+            def _():
+                if turn > 0:
+                    along_z(z_new, mate).wait_recv()
+                for way in range(2):
+                    along_y(way, z_new).start()
+                share(z_new, 0).start()
+
+        if 0 <= turn - 1 < len(order):
+            z_near = z_of_turn(turn - 1)
+
+            @pl.when(has_passages(z_near))
+            def _():
+                for way in range(2):
+                    stat_copy(z_near, (3, 1)[way], whole, stat_recv_y.at[way, z_near], mate).wait_recv()
+                    to_far(way, z_near).start()
+                    share(z_near, (3, 1)[way]).start()
+
+        if 0 <= turn - 2 < len(order):
+            z_far = z_of_turn(turn - 2)
+
+            @pl.when(has_passages(z_far))
+            def _():
+                stat_copy(z_far, 2, whole, stat_recv_far.at[z_far], mate).wait_recv()
+                share(z_far, 2).start()
+
+    def all_shared(count):
+        ref = stats.at[pl.ds(0, count)]
+        return remote(ref, ref, stat_send, stat_recv_mate, mate)
+
+    for core_of, count in ((0, 16), (1, 32)):
+
+        @pl.when(core == core_of)
+        def _():
+            all_shared(count).wait_recv()
 
     def grads_of(slot, carry):
         question = owner[slot]
@@ -419,7 +402,7 @@
     def ring(step, way, chunk):
         return remote(
             send_buf.at[step, way, chunk], recv_buf.at[step, way, chunk],
-            ring_send.at[step, way, chunk], ring_recv.at[step, way, chunk], (x_up, x_down)[way],
+            ring_send, ring_recv.at[step, way, chunk], (x_up, x_down)[way],
         )
 
     def first_chunk(chunk, carry):
@@ -485,42 +468,20 @@
     lax.fori_loop(0, slots_here, finish_slot, 0)
 
     for kind in range(2):
-        for way in range(2):
-            for which in range(3):
-                to_first(kind, way, which, 2 * column).wait_send()
-
-    def drain_second(k, carry):
-        for kind in range(2):
-            for way in range(2):
-                for which in range(3):
-                    to_second(kind, k, way, which, 2 * column).wait_send()
-        return carry
-
-    lax.fori_loop(0, 4, drain_second, 0)
-
-    def drain_mate(k, power):
-        _, _, shard = table(power, first_at, second_at, first_stride, second_stride)
-        for kind in range(2):
-            for half in range(2):
-                to_mate(kind, 2 * shard + half).wait_send()
-        return power * 4
-
-    lax.fori_loop(0, OTHERS, drain_mate, jnp.int32(1))
-    for way in range(2):
-        along_y(way, 0, 0, whole).wait_send()
-        along_y(way, 1, 0, halves[way]).wait_send()
-        for lane_y in range(4):
-            for distance in range(4):
-                along_z(way, lane_y, distance, halves[way] if distance == 3 else whole).wait_send()
-    mate_stats(functools.partial(wait_mate, received=False))
-
-    def drain_ring(chunk, carry):
-        for step in range(3):
-            for way in range(2):
-                ring(step, way, chunk).wait_send()
-        return carry
-
-    lax.fori_loop(0, chunks, drain_ring, 0)
+        ref = blocks.at[kind, core, pl.ds(0, 2 * OTHERS)]
+        for sem in (block_send, mate_send):
+            remote(ref, ref, sem.at[kind], block_recv.at[kind, 0], mate).wait_send()
+    for alone, count in (
+        (core == 0, 63),
+        ((core == 1) & (z_hi == 0), 35),
+        ((core == 1) & (z_hi == 1), 28),
+    ):
+
+        @pl.when(alone)
+        def _():
+            all_shared(count).wait_send()
+
+    remote(send_buf, recv_buf, ring_send, ring_recv.at[0, 0, 0], x_up).wait_send()
 
 
 def on_device(
@@ -562,18 +523,16 @@
             pltpu.VMEM((3, 2, chunks, rows_half, width // chunks), half),
             pltpu.VMEM((chunks, 2 * rows_half, width // chunks), single),
             dma((5,)),
-            dma((2, 2, 3)),
-            dma((2, 4, 2, 3)),
+            dma((2,)),
+            dma((2,)),
             dma((2, 32)),
-            dma((2, 32)),
-            dma((2, 32)),
-            dma((2, 2)),
-            dma((2, 2)),
-            dma((2, 4, 4)),
-            dma((2, 4, 4)),
-            dma((32, 2)),
-            dma((32, 2)),
-            dma((3, 2, chunks)),
+            dma((2, 16)),
+            dma,
+            dma((8,)),
+            dma((2, 8)),
+            dma((8,)),
+            dma,
+            dma,
             dma((3, 2, chunks)),
         ],
         compiler_params=pltpu.CompilerParams(collective_id=0, has_side_effects=True, vmem_limit_bytes=60 << 20),

time: 118 us -> 120 us (1.017)
  Pallas kernels: 117 us -> 119 us
    pallas_call x1, Pallas kernels: 117 us -> 119 us  [on_device(): pl.pallas_call(reader_kernel, out_shape=pltpu.VMEM((slots_here, token_sha...]
where the time goes in v3:
time: 120 us
  Pallas kernels  119 us (99%)
    pallas_call x1, Pallas kernels, on_device(): pl.pallas_call(reader_kernel, out_shape=pltpu.VMEM((slots_here, token_sha...  119 us

profile of v3, /device:TPU:1, one launch (start us, length us, event | category | flops | bytes accessed | tf_op | source)
XLA Modules:
  0.0 120.1 jit_solution(14810235335751864873)
XLA Ops:
  0.0 119.2 %shard_map.91 = bf16[6,16,4096]{2,1,0:T(8,128)(2,1)S(1)} custom-call(s32[32]{0:T(128)} %counts.1, s32[16,32]{1,0:T(8,128)} %bitcast.10, s32[16,32]{1,0:T(8,128)} %bitcast.11, s32[1,32]{1,0:T(1,128)} %bitcast.13, s32[1,32]{1,0:T(1,128)} %bitcast.14, bf16[32,128]{1,0:T(8,128)(2,1)} %bitcast.12, bf16[6,4,16,4096]{3,2,1,0:T(8,128)(2,1)} %bitcast.7, ...), custom_call_target="tpu_custom_call" | custom-call | tf_op jit(solution)/shard_map/pallas_call | solution.py:505
  119.3 0.9 copy.11
